TPU v7x, 32 devices: a whole 2x2x4 slice. The times are simulated.
32 devices in a mesh: groups: 2 (over x), hist: 8 (over z, y), users: 2 (over core).
Axes of the slice: x: 2, y: 2, z: 4, core: 2. Of those that a mesh axis runs over, the one named last changes fastest.
Arguments:
- targets: bfloat16 [4, 512, 1024], P(('groups', 'users'), 'hist'), parts along dimension 0, may hold values from -6 to 6
- hist_keys: bfloat16 [2, 4, 12288, 1024], P(None, ('groups', 'users'), 'hist'), parts along dimension 1, may hold values from -6 to 6
- hist_values: bfloat16 [2, 4, 12288, 1024], P(None, ('groups', 'users'), 'hist'), parts along dimension 1, may hold values from -6 to 6
- lengths: int32 [4], P(('groups', 'users')), parts along dimension 0, may hold values from 3072 to 12288
- cuts: int32 [4, 512], P(('groups', 'users')), parts along dimension 0, may hold values from 1 to 12288
- w_query: bfloat16 [2, 1024, 1024], replicated, may hold values from -0.1875 to 0.1875
- w_gate: bfloat16 [2, 1024, 1024], replicated, may hold values from -0.1875 to 0.1875
- w_out: bfloat16 [2, 1024, 1024], replicated, may hold values from -0.1875 to 0.1875
- ln_gain: float32 [2, 1024], replicated, may hold values from 0.1 to 1.9
Outputs:
- refined: bfloat16 [4, 512, 1024], P(('groups', 'users'), 'hist'), parts along dimension 0
There are 2 independent parts, one for each index of `groups`. A program takes and returns all parts, laid end to end along the dimension named above; an argument that names none is the same for every part. Nothing has to cross between parts.
All inputs are finite; a program needn't handle non-finite values.
Results may differ from a plain program's by a relative error of at most 0.012.
Values may be sent and summed in bfloat16 or wider, within the bound.
A program may use at most 128 MiB of HBM per device.

v0:
```python
import math
import jax
import jax.numpy as jnp
from jax import lax
from jax.sharding import PartitionSpec as P

D = 1024
HEADS = 8
LAYERS = 2


def attend_rows(queries, key_slab, value_slab, limits):
    row_count = queries.shape[0]
    hist_rows = key_slab.shape[0]
    head_size = D // HEADS
    factor = 1.0 / math.sqrt(head_size)
    query_heads = queries.reshape(row_count, HEADS, head_size)
    key_heads = key_slab.reshape(hist_rows, HEADS, head_size)
    value_heads = value_slab.reshape(hist_rows, HEADS, head_size)
    scores = (
        jnp.einsum("rhd,jhd->hrj", query_heads, key_heads, preferred_element_type=jnp.float32)
        * factor
    )
    positions = lax.broadcasted_iota(jnp.int32, (1, row_count, hist_rows), 2)
    visible = positions < limits[None, :, None]
    weights = jnp.where(visible, jax.nn.silu(scores), 0.0).astype(jnp.bfloat16)
    output = jnp.einsum("hrj,jhd->rhd", weights, value_heads, preferred_element_type=jnp.float32)
    return output.reshape(row_count, D)


def finish(hidden, summed, gating, out_weight, gain_row):
    centre = jnp.mean(summed, axis=-1, keepdims=True)
    spread = jnp.mean(jnp.square(summed - centre), axis=-1, keepdims=True)
    normed = ((summed - centre) * lax.rsqrt(spread + 1e-05) * gain_row * gating).astype(
        jnp.bfloat16
    )
    update = jnp.dot(normed, out_weight, preferred_element_type=jnp.float32)
    return (hidden.astype(jnp.float32) + update).astype(jnp.bfloat16)


def per_device(targets, hist_keys, hist_values, lengths, cuts, w_query, w_gate, w_out, ln_gain):
    hist_rows = hist_keys.shape[2]
    offset = lax.axis_index("hist") * hist_rows
    limits = jnp.minimum(cuts[0], lengths[0]) - offset
    hidden = targets[0]
    own_rows = hidden.shape[0]
    for layer_index in range(LAYERS):
        key_slab = hist_keys[layer_index, 0]
        value_slab = hist_values[layer_index, 0]
        queries = jax.nn.silu(
            jnp.dot(hidden, w_query[layer_index], preferred_element_type=jnp.float32)
        ).astype(jnp.bfloat16)
        gating = jax.nn.silu(
            jnp.dot(hidden, w_gate[layer_index], preferred_element_type=jnp.float32)
        )
        all_queries = lax.all_gather(queries, "hist", axis=0, tiled=True)

        def by_block(
            begin_row, row_count, all_queries=all_queries, key_slab=key_slab, value_slab=value_slab
        ):
            return attend_rows(all_queries, key_slab, value_slab, limits)

        summed = lax.psum_scatter(
            by_block(jnp.int32(0), own_rows * lax.axis_size("hist")),
            "hist",
            scatter_dimension=0,
            tiled=True,
        )
        hidden = finish(hidden, summed, gating, w_out[layer_index], ln_gain[layer_index])
    return hidden[None]


def solution(mesh):
    return jax.shard_map(
        per_device,
        mesh=mesh,
        in_specs=(
            P(("groups", "users"), "hist", None),
            P(None, ("groups", "users"), "hist", None),
            P(None, ("groups", "users"), "hist", None),
            P(("groups", "users")),
            P(("groups", "users"), None),
            P(),
            P(),
            P(),
            P(),
        ),
        out_specs=P(("groups", "users"), "hist", None),
        check_vma=False,
    )
```

profile of v0, /device:TPU:0, one launch (start us, length us, event | category | flops | bytes accessed | tf_op | source)
XLA Modules:
  0.0 282.8 jit_solution(4211287939097694233)
XLA Ops:
  6.5 0.0 all-gather.3.cloned.1.call-start
  6.5 2.8 %multiply_convert_fusion.3 = bf16[64,1024]{1,0:T(8,128)(2,1)} fusion(bf16[2,1024,1024]{2,1,0:T(8,128)(2,1)} %param.14, bf16[1,64,1024]{2,1,0:T(8,128)(2,1)} %param.9), kind=kOutput, calls=%fused_computation.41 | convolution fusion | flops 134545408 | bytes 2359296 | tf_op jit(solution)/shard_map/dot_general | solution.py:51
  9.4 0.0 all-gather.3.cloned.1.call-update
  9.4 0.0 reduce-scatter.3.cloned.1.call-start
  9.5 5.2 %fusion.80 = (bf16[1,1,1536,1024]{3,2,1,0:T(8,128)(2,1)S(1)}, bf16[1,1,1536,1024]{3,2,1,0:T(8,128)(2,1)}) fusion(bf16[2,1,1536,1024]{3,2,1,0:T(8,128)(2,1)} %param.10), kind=kLoop, calls=%fused_computation.67 | loop fusion | bytes 12582912 | tf_op jit(solution)/shard_map/slice | solution.py:48
  14.7 4.7 %copy.30 = bf16[1,1,1536,1024]{2,3,1,0:T(8,128)(2,1)} copy(bf16[1,1,1536,1024]{3,2,1,0:T(8,128)(2,1)} %get-tuple-element.6) | data formatting | bytes 6291456
  19.3 6.2 %fusion.81 = (bf16[1,1,1536,1024]{3,2,1,0:T(8,128)(2,1)}, bf16[1,1,1536,1024]{3,2,1,0:T(8,128)(2,1)}) fusion(bf16[2,1,1536,1024]{3,2,1,0:T(8,128)(2,1)} %param.11), kind=kLoop, calls=%fused_computation.68 | loop fusion | bytes 12582912 | tf_op jit(solution)/shard_map/slice | solution.py:49
  25.6 0.0 copy-start.2
  25.6 4.7 %copy.19 = bf16[1,1,1536,1024]{2,3,1,0:T(8,128)(2,1)} copy(bf16[1,1,1536,1024]{3,2,1,0:T(8,128)(2,1)} %get-tuple-element.8) | data formatting | bytes 6291456 | tf_op jit(solution)/shard_map/slice | solution.py:49
  30.9 0.0 copy-done.2
  31.0 1.4 iota_compare_fusion
  32.4 20.2 %all-gather.3.cloned.1.call-done = bf16[512,1024]{1,0:T(8,128)(2,1)} async-done(((bf16[64,1024]{1,0:T(8,128)(2,1)}), bf16[512,1024]{1,0:T(8,128)(2,1)}) %all-gather.3.cloned.1.call-update) | async-done | bytes 1048592 | tf_op jit(solution)/shard_map/all_gather | solution.py:56
  52.6 15.0 %fusion = f32[8,512,128]{1,2,0:T(8,128)} fusion(bf16[1536,8,128]{0,2,1:T(8,128)(2,1)} %bitcast.88, bf16[1536,8,128]{0,2,1:T(8,128)(2,1)} %bitcast.87, pred[512,1536]{1,0:T(8,128)(4,1)} %iota_compare_fusion, bf16[512,1024]{1,0:T(8,128)(2,1)} %all-gather.3.cloned.1.call-done), kind=kOutput, calls=%fused_computation.3 | convolution fusion | flops 3265265664 | bytes 10223616 | tf_op jit(solution)/shard_map/hrj,jhd->rhd/dot_general | solution.py:27
  67.6 0.0 copy-start.1
  67.6 0.0 copy-start.3
  67.6 3.0 %copy.28 = f32[512,1024]{1,0:T(8,128)} copy(f32[512,1024]{0,1:T(8,128)} %bitcast.92) | data formatting | bytes 4194304 | tf_op jit(solution)/shard_map/reshape | solution.py:28
  70.6 0.0 reduce-scatter.3.cloned.1.call-update
  70.6 0.0 all-gather.5.cloned.1.call-start
  70.7 0.0 copy-done.1
  70.7 67.1 %reduce-scatter.3.cloned.1.call-done = f32[64,1024]{1,0:T(8,128)} async-done(((f32[512,1024]{1,0:T(8,128)}), f32[64,1024]{1,0:T(8,128)}) %reduce-scatter.3.cloned.1.call-update) | async-done | bytes 262160 | tf_op jit(solution)/shard_map/reduce_scatter | solution.py:63
  137.7 1.1 reduce_sum.36
  138.8 1.1 multiply_reduce_fusion.1
  140.0 0.0 copy-done.3
  140.0 3.2 %fusion.29 = bf16[64,1024]{1,0:T(8,128)(2,1)S(1)} fusion(bf16[2,1024,1024]{2,1,0:T(8,128)(2,1)} %param.16, bf16[2,1024,1024]{2,1,0:T(8,128)(2,1)} %param.15, f32[64,1024]{1,0:T(8,128)} %reduce-scatter.3.cloned.1.call-done, bf16[1,64,1024]{2,1,0:T(8,128)(2,1)S(1)} %copy-done.3, f32[1024]{0:T(1024)S(1)} %bitcast.95, f32[64]{0:T(128)S(1)} %add_rsqrt_fusion.1, ...), kind=kOutput, calls=%fused_computation.26 | convolution fusion | flops 269221888 | bytes 4854784 | tf_op jit(solution)/shard_map/dot_general | solution.py:37
  143.2 2.8 multiply_convert_fusion.1
  146.0 0.0 all-gather.5.cloned.1.call-update
  146.0 0.2 reduce-scatter.5.cloned.1.call-start
  146.2 3.0 %copy.31 = bf16[1,1,1536,1024]{2,3,1,0:T(8,128)(2,1)} copy(bf16[1,1,1536,1024]{3,2,1,0:T(8,128)(2,1)S(1)} %get-tuple-element.5) | data formatting | bytes 6291456
  149.2 0.0 copy-start
  149.3 4.8 %copy.24 = bf16[1,1,1536,1024]{2,3,1,0:T(8,128)(2,1)} copy(bf16[1,1,1536,1024]{3,2,1,0:T(8,128)(2,1)} %get-tuple-element.7) | data formatting | bytes 6291456 | tf_op jit(solution)/shard_map/slice | solution.py:49
  154.1 31.4 %all-gather.5.cloned.1.call-done = bf16[512,1024]{1,0:T(8,128)(2,1)} async-done(((bf16[64,1024]{1,0:T(8,128)(2,1)}), bf16[512,1024]{1,0:T(8,128)(2,1)}) %all-gather.5.cloned.1.call-update) | async-done | bytes 1048592 | tf_op jit(solution)/shard_map/all_gather | solution.py:56
  185.5 0.0 copy-done
  185.5 14.6 %fusion.1 = f32[8,512,128]{1,2,0:T(8,128)} fusion(bf16[1536,8,128]{0,2,1:T(8,128)(2,1)} %bitcast.90, bf16[1536,8,128]{0,2,1:T(8,128)(2,1)S(1)} %bitcast.89, pred[512,1536]{1,0:T(8,128)(4,1)} %iota_compare_fusion, bf16[512,1024]{1,0:T(8,128)(2,1)} %all-gather.5.cloned.1.call-done), kind=kOutput, calls=%fused_computation.4 | convolution fusion | flops 3265265664 | bytes 10223616 | tf_op jit(solution)/shard_map/hrj,jhd->rhd/dot_general | solution.py:27
  200.1 2.9 %copy.29 = f32[512,1024]{1,0:T(8,128)} copy(f32[512,1024]{0,1:T(8,128)} %bitcast.91) | data formatting | bytes 4194304 | tf_op jit(solution)/shard_map/reshape | solution.py:28
  203.0 0.0 reduce-scatter.5.cloned.1.call-update
  203.0 67.1 %reduce-scatter.5.cloned.1.call-done = f32[64,1024]{1,0:T(8,128)} async-done(((f32[512,1024]{1,0:T(8,128)}), f32[64,1024]{1,0:T(8,128)}) %reduce-scatter.5.cloned.1.call-update) | async-done | bytes 262160 | tf_op jit(solution)/shard_map/reduce_scatter | solution.py:63
  270.1 1.1 reduce_sum.38
  271.2 1.1 multiply_reduce_fusion
  272.4 3.9 %fusion.32 = bf16[1,64,1024]{2,1,0:T(8,128)(2,1)} fusion(bf16[2,1024,1024]{2,1,0:T(8,128)(2,1)} %param.16, bf16[64,1024]{1,0:T(8,128)(2,1)S(1)} %fusion.29, bf16[2,1024,1024]{2,1,0:T(8,128)(2,1)} %param.15, f32[64,1024]{1,0:T(8,128)} %reduce-scatter.5.cloned.1.call-done, f32[1024]{0:T(1024)S(1)} %bitcast.94, f32[64]{0:T(128)S(1)} %add_rsqrt_fusion, ...), kind=kOutput, calls=%fused_computation.27 | convolution fusion | flops 269221888 | bytes 4854784 | tf_op jit(solution)/shard_map/dot_general | solution.py:37
  (6 shorter events, 0.0 us)
Async XLA Ops:
  6.5 46.0 %all-gather.3.cloned.1.call-start = ((), (), s32[]{:S(2)}) async-start(), calls=%async_computation.2 | async-start | bytes 1179648 | tf_op jit(solution)/shard_map/all_gather | solution.py:56
  9.4 128.3 %reduce-scatter.3.cloned.1.call-start = ((), (), s32[]{:S(2)}) async-start(), calls=%async_computation.3 | async-start | bytes 2359296 | tf_op jit(solution)/shard_map/reduce_scatter | solution.py:63
  25.6 5.4 %copy-start.2 = (s32[1,512]{1,0:T(1,128)S(1)}, s32[1,512]{1,0:T(1,128)}, u32[]{:S(2)}) copy-start(s32[1,512]{1,0:T(1,128)} %param.13) | copy-start | bytes 6148
  67.6 3.1 %copy-start.1 = (f32[2,1024]{1,0:T(2,128)S(1)}, f32[2,1024]{1,0:T(2,128)}, u32[]{:S(2)}) copy-start(f32[2,1024]{1,0:T(2,128)} %param.17) | copy-start | bytes 24580
  67.6 72.4 %copy-start.3 = (bf16[1,64,1024]{2,1,0:T(8,128)(2,1)S(1)}, bf16[1,64,1024]{2,1,0:T(8,128)(2,1)}, u32[]{:S(2)}) copy-start(bf16[1,64,1024]{2,1,0:T(8,128)(2,1)} %param.9) | copy-start | bytes 393220
  70.6 114.9 %all-gather.5.cloned.1.call-start = ((), (), s32[]{:S(2)}) async-start(), calls=%async_computation.4 | async-start | bytes 1179648 | tf_op jit(solution)/shard_map/all_gather | solution.py:56
  146.0 124.1 %reduce-scatter.5.cloned.1.call-start = ((), (), s32[]{:S(2)}) async-start(), calls=%async_computation.5 | async-start | bytes 2359296 | tf_op jit(solution)/shard_map/reduce_scatter | solution.py:63
  149.2 36.3 %copy-start = (bf16[1,1,1536,1024]{2,3,1,0:T(8,128)(2,1)S(1)}, bf16[1,1,1536,1024]{2,3,1,0:T(8,128)(2,1)}, u32[]{:S(2)}) copy-start(bf16[1,1,1536,1024]{2,3,1,0:T(8,128)(2,1)} %copy.31) | copy-start | bytes 9437188
Sparse Core Ops, SparseCore 0:
  9.5 42.9 all-gather.2
  70.7 66.9 reduce-scatter.2
  146.1 39.3 all-gather.4
  203.2 66.9 reduce-scatter.4
where the time goes:
time: 283 us
  waiting for transfers between devices  186 us (66%)
  matrix products  42.3 us (15%)
  local copies, waits for them, and re-layouts  34.6 us (12%)
  between operations  13.9 us (5%)
  other arithmetic  5.86 us (2%)
    reduce_scatter x2, waiting for transfers between devices, per_device(): lax.psum_scatter(by_block(jnp.int32(0), own_rows * lax.axis_size('hist'))...  134 us
    all_gather x2, waiting for transfers between devices, per_device(): all_queries = lax.all_gather(queries, 'hist', axis=0, tiled=True)  51.6 us
    dot_general x2, matrix products, attend_rows(): jnp.einsum('hrj,jhd->rhd', weights, value_heads, preferred_element_type=j...  29.6 us
    slice x3, local copies, waits for them, and re-layouts, per_device(): value_slab = hist_values[layer_index, 0]  15.8 us
    unnamed x10, local copies, waits for them, and re-layouts  7.69 us
    dot_general x2, matrix products, finish(): update = jnp.dot(normed, out_weight, preferred_element_type=jnp.float32)  7.08 us
    reshape x2, local copies, waits for them, and re-layouts, attend_rows(): return output.reshape(row_count, D)  5.88 us
  transfers between devices with their start and end apart: 4, of which 4 were waited for; matrix products, arithmetic and copies ran while one was open for 11% of the time, Pallas kernels for 0%

commit v1 on v0

--- a/solution.py
+++ b/solution.py
@@ -53,7 +53,9 @@
         gating = jax.nn.silu(
             jnp.dot(hidden, w_gate[layer_index], preferred_element_type=jnp.float32)
         )
-        all_queries = lax.all_gather(queries, "hist", axis=0, tiled=True)
+        all_queries = jnp.concatenate(
+            lax.all_to_all(jnp.stack([queries] * lax.axis_size("hist")), "hist", 0, 0), axis=0
+        )
 
         def by_block(
             begin_row, row_count, all_queries=all_queries, key_slab=key_slab, value_slab=value_slab

time: 283 us -> 271 us (0.958)
  waiting for transfers between devices: 186 us -> 155 us
  starting transfers between devices: 0.31 us -> 11.8 us
  local copies, waits for them, and re-layouts: 34.6 us -> 41.7 us
    all_gather x2 -> x0, waiting for transfers between devices: 51.6 us -> none  [per_device(): all_queries = lax.all_gather(queries, 'hist', axis=0, tiled=True)]
    all_to_all x0 -> x2, waiting for transfers between devices: none -> 19.6 us  [per_device(): lax.all_to_all(jnp.stack([queries] * lax.axis_size('hist')), 'hist', 0, 0)]
    all_to_all x0 -> x2, starting transfers between devices: none -> 11.6 us  [per_device(): lax.all_to_all(jnp.stack([queries] * lax.axis_size('hist')), 'hist', 0, 0)]
    unnamed x10 -> x12, local copies, waits for them, and re-layouts: 7.69 us -> 12.7 us
where the time goes in v1:
time: 271 us; the launch traced here: 270 us
  waiting for transfers between devices  155 us (57%)
  local copies, waits for them, and re-layouts  41.7 us (15%)
  matrix products  41.5 us (15%)
  between operations  14.2 us (5%)
  starting transfers between devices  11.8 us (4%)
  other arithmetic  5.86 us (2%)
    reduce_scatter x2, waiting for transfers between devices, per_device(): lax.psum_scatter(by_block(jnp.int32(0), own_rows * lax.axis_size('hist'))...  135 us
    dot_general x2, matrix products, attend_rows(): jnp.einsum('hrj,jhd->rhd', weights, value_heads, preferred_element_type=j...  30.1 us
    all_to_all x2, waiting for transfers between devices, per_device(): lax.all_to_all(jnp.stack([queries] * lax.axis_size('hist')), 'hist', 0, 0)  19.6 us
    slice x3, local copies, waits for them, and re-layouts, per_device(): value_slab = hist_values[layer_index, 0]  15.7 us
    unnamed x12, local copies, waits for them, and re-layouts  12.7 us
    all_to_all x2, starting transfers between devices, per_device(): lax.all_to_all(jnp.stack([queries] * lax.axis_size('hist')), 'hist', 0, 0)  11.6 us
    dot_general x2, matrix products, finish(): update = jnp.dot(normed, out_weight, preferred_element_type=jnp.float32)  7.1 us
    reshape x2, local copies, waits for them, and re-layouts, attend_rows(): return output.reshape(row_count, D)  5.89 us
  transfers between devices with their start and end apart: 4, of which 4 were waited for; matrix products, arithmetic and copies ran while one was open for 11% of the time, Pallas kernels for 0%

profile of v1, /device:TPU:0, one launch (start us, length us, event | category | flops | bytes accessed | tf_op | source)
XLA Modules:
  0.0 270.0 jit_solution(16566628069464908697)
XLA Ops:
  6.5 2.2 multiply_convert_fusion.3
  8.7 1.1 stack.4
  9.8 7.3 %all-to-all-start = ((bf16[8,64,1024]{2,1,0:T(8,128)(2,1)}), bf16[8,64,1024]{2,1,0:T(8,128)(2,1)}, u32[]{:S(2)}, u32[]{:S(2)}) async-start(bf16[8,64,1024]{2,1,0:T(8,128)(2,1)} %stack.4), calls=%async_computation | async-start | bytes 2097152 | tf_op jit(solution)/shard_map/all_to_all | solution.py:57
  17.1 0.0 reduce-scatter.3.cloned.1.call-start
  17.2 5.2 %fusion.76 = (bf16[1,1,1536,1024]{3,2,1,0:T(8,128)(2,1)S(1)}, bf16[1,1,1536,1024]{3,2,1,0:T(8,128)(2,1)}) fusion(bf16[2,1,1536,1024]{3,2,1,0:T(8,128)(2,1)} %param.10), kind=kLoop, calls=%fused_computation.65 | loop fusion | bytes 12582912 | tf_op jit(solution)/shard_map/slice | solution.py:48
  22.4 4.7 %copy.28 = bf16[1,1,1536,1024]{2,3,1,0:T(8,128)(2,1)} copy(bf16[1,1,1536,1024]{3,2,1,0:T(8,128)(2,1)} %get-tuple-element.6) | data formatting | bytes 6291456
  27.1 6.1 %fusion.77 = (bf16[1,1,1536,1024]{3,2,1,0:T(8,128)(2,1)}, bf16[1,1,1536,1024]{3,2,1,0:T(8,128)(2,1)}) fusion(bf16[2,1,1536,1024]{3,2,1,0:T(8,128)(2,1)} %param.11), kind=kLoop, calls=%fused_computation.66 | loop fusion | bytes 12582912 | tf_op jit(solution)/shard_map/slice | solution.py:49
  33.2 0.0 copy-start.2
  33.2 4.7 %copy.17 = bf16[1,1,1536,1024]{2,3,1,0:T(8,128)(2,1)} copy(bf16[1,1,1536,1024]{3,2,1,0:T(8,128)(2,1)} %get-tuple-element.8) | data formatting | bytes 6291456 | tf_op jit(solution)/shard_map/slice | solution.py:49
  38.6 0.0 copy-done.2
  38.6 1.4 iota_compare_fusion
  40.0 3.0 %all-to-all-done = bf16[8,64,1024]{2,1,0:T(8,128)(2,1)} async-done(((bf16[8,64,1024]{2,1,0:T(8,128)(2,1)}), bf16[8,64,1024]{2,1,0:T(8,128)(2,1)}, u32[]{:S(2)}, u32[]{:S(2)}) %all-to-all-start) | async-done | bytes 1048608 | tf_op jit(solution)/shard_map/all_to_all | solution.py:57
  43.0 2.5 copy.30
  45.5 15.3 %fusion = f32[8,512,128]{1,2,0:T(8,128)} fusion(bf16[1536,8,128]{0,2,1:T(8,128)(2,1)} %bitcast.76, bf16[1536,8,128]{0,2,1:T(8,128)(2,1)} %bitcast.75, pred[512,1536]{1,0:T(8,128)(4,1)} %iota_compare_fusion, bf16[512,8,128]{2,1,0:T(8,128)(2,1)} %bitcast.82), kind=kOutput, calls=%fused_computation.3 | convolution fusion | flops 3265265664 | bytes 10223616 | tf_op jit(solution)/shard_map/hrj,jhd->rhd/dot_general | solution.py:27
  60.8 0.0 copy-start.1
  60.8 0.0 copy-start.3
  60.8 3.0 %copy.26 = f32[512,1024]{1,0:T(8,128)} copy(f32[512,1024]{0,1:T(8,128)} %bitcast.80) | data formatting | bytes 4194304 | tf_op jit(solution)/shard_map/reshape | solution.py:28
  63.8 0.0 reduce-scatter.3.cloned.1.call-update
  63.8 0.0 copy-done.1
  63.8 67.5 %reduce-scatter.3.cloned.1.call-done = f32[64,1024]{1,0:T(8,128)} async-done(((f32[512,1024]{1,0:T(8,128)}), f32[64,1024]{1,0:T(8,128)}) %reduce-scatter.3.cloned.1.call-update) | async-done | bytes 262160 | tf_op jit(solution)/shard_map/reduce_scatter | solution.py:65
  131.3 1.1 reduce_sum.36
  132.4 1.1 multiply_reduce_fusion.1
  133.5 0.0 copy-done.3
  133.5 3.2 %fusion.29 = bf16[64,1024]{1,0:T(8,128)(2,1)S(1)} fusion(bf16[2,1024,1024]{2,1,0:T(8,128)(2,1)} %param.16, bf16[2,1024,1024]{2,1,0:T(8,128)(2,1)} %param.15, f32[64,1024]{1,0:T(8,128)} %reduce-scatter.3.cloned.1.call-done, bf16[1,64,1024]{2,1,0:T(8,128)(2,1)S(1)} %copy-done.3, f32[1024]{0:T(1024)S(1)} %bitcast.85, f32[64]{0:T(128)S(1)} %add_rsqrt_fusion.1, ...), kind=kOutput, calls=%fused_computation.26 | convolution fusion | flops 269221888 | bytes 4854784 | tf_op jit(solution)/shard_map/dot_general | solution.py:37
  136.7 2.1 multiply_convert_fusion.1
  138.9 1.1 stack.5
  140.0 4.2 %all-to-all-start.1 = ((bf16[8,64,1024]{2,1,0:T(8,128)(2,1)}), bf16[8,64,1024]{2,1,0:T(8,128)(2,1)}, u32[]{:S(2)}, u32[]{:S(2)}) async-start(bf16[8,64,1024]{2,1,0:T(8,128)(2,1)} %stack.5), calls=%async_computation.2 | async-start | bytes 2097152 | tf_op jit(solution)/shard_map/all_to_all | solution.py:57
  144.2 0.2 reduce-scatter.5.cloned.1.call-start
  144.4 3.0 %copy.29 = bf16[1,1,1536,1024]{2,3,1,0:T(8,128)(2,1)} copy(bf16[1,1,1536,1024]{3,2,1,0:T(8,128)(2,1)S(1)} %get-tuple-element.5) | data formatting | bytes 6291456
  147.5 0.0 copy-start
  147.5 4.8 %copy.22 = bf16[1,1,1536,1024]{2,3,1,0:T(8,128)(2,1)} copy(bf16[1,1,1536,1024]{3,2,1,0:T(8,128)(2,1)} %get-tuple-element.7) | data formatting | bytes 6291456 | tf_op jit(solution)/shard_map/slice | solution.py:49
  152.3 16.7 %all-to-all-done.1 = bf16[8,64,1024]{2,1,0:T(8,128)(2,1)} async-done(((bf16[8,64,1024]{2,1,0:T(8,128)(2,1)}), bf16[8,64,1024]{2,1,0:T(8,128)(2,1)}, u32[]{:S(2)}, u32[]{:S(2)}) %all-to-all-start.1) | async-done | bytes 1048608 | tf_op jit(solution)/shard_map/all_to_all | solution.py:57
  169.0 2.5 copy.31
  171.5 0.0 copy-done
  171.5 14.8 %fusion.1 = f32[8,512,128]{1,2,0:T(8,128)} fusion(bf16[1536,8,128]{0,2,1:T(8,128)(2,1)} %bitcast.78, bf16[1536,8,128]{0,2,1:T(8,128)(2,1)S(1)} %bitcast.77, pred[512,1536]{1,0:T(8,128)(4,1)} %iota_compare_fusion, bf16[512,8,128]{2,1,0:T(8,128)(2,1)} %bitcast.81), kind=kOutput, calls=%fused_computation.4 | convolution fusion | flops 3265265664 | bytes 10223616 | tf_op jit(solution)/shard_map/hrj,jhd->rhd/dot_general | solution.py:27
  186.3 2.9 %copy.27 = f32[512,1024]{1,0:T(8,128)} copy(f32[512,1024]{0,1:T(8,128)} %bitcast.79) | data formatting | bytes 4194304 | tf_op jit(solution)/shard_map/reshape | solution.py:28
  189.2 0.0 reduce-scatter.5.cloned.1.call-update
  189.2 67.8 %reduce-scatter.5.cloned.1.call-done = f32[64,1024]{1,0:T(8,128)} async-done(((f32[512,1024]{1,0:T(8,128)}), f32[64,1024]{1,0:T(8,128)}) %reduce-scatter.5.cloned.1.call-update) | async-done | bytes 262160 | tf_op jit(solution)/shard_map/reduce_scatter | solution.py:65
  257.0 1.1 reduce_sum.38
  258.1 1.1 multiply_reduce_fusion
  259.2 3.9 %fusion.32 = bf16[1,64,1024]{2,1,0:T(8,128)(2,1)} fusion(bf16[2,1024,1024]{2,1,0:T(8,128)(2,1)} %param.16, bf16[64,1024]{1,0:T(8,128)(2,1)S(1)} %fusion.29, bf16[2,1024,1024]{2,1,0:T(8,128)(2,1)} %param.15, f32[64,1024]{1,0:T(8,128)} %reduce-scatter.5.cloned.1.call-done, f32[1024]{0:T(1024)S(1)} %bitcast.84, f32[64]{0:T(128)S(1)} %add_rsqrt_fusion, ...), kind=kOutput, calls=%fused_computation.27 | convolution fusion | flops 269221888 | bytes 4854784 | tf_op jit(solution)/shard_map/dot_general | solution.py:37
  (6 shorter events, 0.0 us)
Async XLA Ops:
  9.8 33.2 %all-to-all-start = ((bf16[8,64,1024]{2,1,0:T(8,128)(2,1)}), bf16[8,64,1024]{2,1,0:T(8,128)(2,1)}, u32[]{:S(2)}, u32[]{:S(2)}) async-start(bf16[8,64,1024]{2,1,0:T(8,128)(2,1)} %stack.4), calls=%async_computation | async-start | bytes 2097152 | tf_op jit(solution)/shard_map/all_to_all | solution.py:57
  17.1 114.1 %reduce-scatter.3.cloned.1.call-start = ((), (), s32[]{:S(2)}) async-start(), calls=%async_computation.4 | async-start | bytes 2359296 | tf_op jit(solution)/shard_map/reduce_scatter | solution.py:65
  33.2 5.4 %copy-start.2 = (s32[1,512]{1,0:T(1,128)S(1)}, s32[1,512]{1,0:T(1,128)}, u32[]{:S(2)}) copy-start(s32[1,512]{1,0:T(1,128)} %param.13) | copy-start | bytes 6148
  60.8 3.0 %copy-start.1 = (f32[2,1024]{1,0:T(2,128)S(1)}, f32[2,1024]{1,0:T(2,128)}, u32[]{:S(2)}) copy-start(f32[2,1024]{1,0:T(2,128)} %param.17) | copy-start | bytes 24580
  60.8 72.8 %copy-start.3 = (bf16[1,64,1024]{2,1,0:T(8,128)(2,1)S(1)}, bf16[1,64,1024]{2,1,0:T(8,128)(2,1)}, u32[]{:S(2)}) copy-start(bf16[1,64,1024]{2,1,0:T(8,128)(2,1)} %param.9) | copy-start | bytes 393220
  140.0 29.0 %all-to-all-start.1 = ((bf16[8,64,1024]{2,1,0:T(8,128)(2,1)}), bf16[8,64,1024]{2,1,0:T(8,128)(2,1)}, u32[]{:S(2)}, u32[]{:S(2)}) async-start(bf16[8,64,1024]{2,1,0:T(8,128)(2,1)} %stack.5), calls=%async_computation.2 | async-start | bytes 2097152 | tf_op jit(solution)/shard_map/all_to_all | solution.py:57
  144.2 112.8 %reduce-scatter.5.cloned.1.call-start = ((), (), s32[]{:S(2)}) async-start(), calls=%async_computation.5 | async-start | bytes 2359296 | tf_op jit(solution)/shard_map/reduce_scatter | solution.py:65
  147.5 24.0 %copy-start = (bf16[1,1,1536,1024]{2,3,1,0:T(8,128)(2,1)S(1)}, bf16[1,1,1536,1024]{2,3,1,0:T(8,128)(2,1)}, u32[]{:S(2)}) copy-start(bf16[1,1,1536,1024]{2,3,1,0:T(8,128)(2,1)} %copy.29) | copy-start | bytes 9437188
Sparse Core Ops, SparseCore 0:
  63.9 67.3 reduce-scatter.2
  189.3 67.6 reduce-scatter.4
